TPU v7x, 32 devices: a whole 2x2x4 slice. The times are simulated.
32 devices in a mesh: fsdp: 2 (over x), ctx: 4 (over z), tp: 4 (over y, core).
Axes of the slice: x: 2, y: 2, z: 4, core: 2. Of those that a mesh axis runs over, the one named last changes fastest.
Arguments:
- tokens: bfloat16 [8192, 1024], P(('fsdp', 'ctx')), may hold values from -6 to 6
- w_qkv: bfloat16 [3, 1024, 1024], P(None, 'fsdp', 'tp'), may hold values from -0.25 to 0.25
- w_out: bfloat16 [1024, 1024], P('tp', 'fsdp'), may hold values from -0.75 to 0.75
- w_up: bfloat16 [1024, 4096], P('fsdp', 'tp'), may hold values from -0.1875 to 0.1875
- w_down: bfloat16 [4096, 1024], P('tp', 'fsdp'), may hold values from -0.09375 to 0.09375
- gains: bfloat16 [2, 1024], P(None, 'fsdp'), may hold values from 0.5 to 1.5
- shifts: bfloat16 [2, 1024], P(None, 'fsdp'), may hold values from -3 to 3
- lengths: int32 [2, 3], P('fsdp'), may hold values from 256 to 2048, as said below
- out_grad: bfloat16 [8192, 1024], P(('fsdp', 'ctx')), may hold values from -6 to 6
Outputs:
- out: bfloat16 [8192, 1024], P(('fsdp', 'ctx'))
- input_grad: bfloat16 [8192, 1024], P(('fsdp', 'ctx'))
- grad_qkv: float32 [3, 1024, 1024], P(None, 'fsdp', 'tp')
- grad_out: float32 [1024, 1024], P('tp', 'fsdp')
- grad_up: float32 [1024, 4096], P('fsdp', 'tp')
- grad_down: float32 [4096, 1024], P('tp', 'fsdp')
- grad_gains: float32 [2, 1024], P(None, 'fsdp')
- grad_shifts: float32 [2, 1024], P(None, 'fsdp')
Inputs may be any that keep to these rules, and one draw needn't show every extreme that they name: `lengths`: in each row one sequence has exactly 2048 tokens and the others 2048 // 8 to 1024; sequences lie end to end from the pack's first slot, and the slots after them up to 4096 are padding.
All inputs are finite; a program needn't handle non-finite values.
Results may differ from a plain program's by a relative error of at most 0.014.
The roundings to bfloat16 on the way count: a program that leaves them out, or rounds other values in their place, can miss the bound.
Values may be sent and summed in bfloat16 or wider, within the bound.
No kernel may reach another device: no remote copies, remote signals or barrier semaphores. Data moves between devices by JAX's collectives and lax.ppermute only.
A program may use at most 192 MiB of HBM per device.

v0:
```python
import math
import jax
import jax.numpy as jnp
from jax import lax
from jax.sharding import PartitionSpec as P

HEAD_DIM = 64
SEQS = 3
norm_eps = 1e-12
masked_low = -1e30


def layer_norm(rows, gain, shift):
    centre = rows - jnp.mean(rows, axis=-1, keepdims=True)
    spread = jnp.mean(centre * centre, axis=-1, keepdims=True)
    return centre * lax.rsqrt(spread + norm_eps) * gain + shift


def exact_gelu(values):
    return jax.nn.gelu(values, approximate=False)


def contract_rows(left, right):
    return lax.dot_general(
        left, right, (((0,), (0,)), ((), ())), preferred_element_type=jnp.float32
    )


def contract_cols(left, right):
    return lax.dot_general(
        left, right, (((1,), (1,)), ((), ())), preferred_element_type=jnp.float32
    )


def tp_total(terms):
    return lax.psum(terms, "tp")


def segment_of(lengths_row, total):
    seq_ends = jnp.cumsum(lengths_row)
    positions = jnp.arange(total, dtype=jnp.int32)
    return jnp.sum((positions[:, None] >= seq_ends[None, :]).astype(jnp.int32), axis=1)


def score_block(query_block, seg_block, key_heads, segments):
    raw_scores = jnp.einsum(
        "qhd,khd->hqk", query_block, key_heads, preferred_element_type=jnp.float32
    )
    allowed = (seg_block[:, None] == segments[None, :]) & (segments[None, :] < SEQS)
    return (raw_scores * (1.0 / math.sqrt(HEAD_DIM)), allowed)


def attend_forward(query_heads, seg_mine, key_heads, value_heads, segments):

    def one_block(inputs):
        query_block, seg_block = inputs
        scores, allowed = score_block(query_block, seg_block, key_heads, segments)
        has_key = jnp.any(allowed, axis=1)
        masked = jnp.where(allowed[None], scores, masked_low)
        row_max = jnp.where(has_key[None, :, None], jnp.max(masked, axis=2, keepdims=True), 0.0)
        exp_terms = jnp.where(allowed[None], jnp.exp(masked - row_max), 0.0)
        denominator = (
            jnp.sum(exp_terms, axis=2, keepdims=True)
            + (1.0 - has_key.astype(jnp.float32))[None, :, None]
        )
        attn_probs = (exp_terms / denominator).astype(jnp.bfloat16)
        context = jnp.einsum(
            "hqk,khd->qhd", attn_probs, value_heads, preferred_element_type=jnp.float32
        )
        log_total = row_max[:, :, 0] + jnp.log(denominator[:, :, 0])
        return (context.astype(jnp.bfloat16), log_total)

    return lax.map(one_block, (query_heads, seg_mine))


def attend_backward(
    query_heads, seg_mine, grad_heads, log_totals, key_heads, value_heads, segments
):
    score_scale = 1.0 / math.sqrt(HEAD_DIM)
    zero_keys = jnp.zeros(key_heads.shape, jnp.float32)

    def one_block(carry, inputs):
        key_grad, value_grad = carry
        query_block, seg_block, grad_block, log_block = inputs
        scores, allowed = score_block(query_block, seg_block, key_heads, segments)
        attn_probs = jnp.where(allowed[None], jnp.exp(scores - log_block[:, :, None]), 0.0)
        probs_low = attn_probs.astype(jnp.bfloat16)
        grad_probs = jnp.einsum(
            "qhd,khd->hqk", grad_block, value_heads, preferred_element_type=jnp.float32
        )
        row_delta = jnp.sum(attn_probs * grad_probs, axis=2, keepdims=True)
        grad_scores = (attn_probs * (grad_probs - row_delta) * score_scale).astype(jnp.bfloat16)
        query_grad = jnp.einsum(
            "hqk,khd->qhd", grad_scores, key_heads, preferred_element_type=jnp.float32
        )
        key_grad = key_grad + jnp.einsum(
            "hqk,qhd->khd", grad_scores, query_block, preferred_element_type=jnp.float32
        )
        value_grad = value_grad + jnp.einsum(
            "hqk,qhd->khd", probs_low, grad_block, preferred_element_type=jnp.float32
        )
        return ((key_grad, value_grad), query_grad)

    return lax.scan(
        one_block, (zero_keys, zero_keys), (query_heads, seg_mine, grad_heads, log_totals)
    )


def body(tokens, w_qkv, w_out, w_up, w_down, gains, shifts, lengths, out_grad):
    full_qkv, full_out, full_up, full_down, full_gains, full_shifts = (
        lax.all_gather(w_qkv, "fsdp", axis=1, tiled=True),
        lax.all_gather(w_out, "fsdp", axis=1, tiled=True),
        lax.all_gather(w_up, "fsdp", axis=0, tiled=True),
        lax.all_gather(w_down, "fsdp", axis=1, tiled=True),
        lax.all_gather(gains, "fsdp", axis=1, tiled=True),
        lax.all_gather(shifts, "fsdp", axis=1, tiled=True),
    )
    tok_rows = tokens.shape[0]
    local_width = full_qkv.shape[2]
    local_heads = local_width // HEAD_DIM
    block_rows = min(512, tok_rows)
    block_count = tok_rows // block_rows
    pack_rows = tok_rows * lax.axis_size("ctx")
    segments = segment_of(lengths[0], pack_rows)
    seg_mine = lax.dynamic_slice_in_dim(
        segments, lax.axis_index("ctx") * tok_rows, tok_rows
    ).reshape(block_count, block_rows)
    residual_in = tokens.astype(jnp.float32)
    projected = jnp.einsum(
        "td,sdc->stc", tokens, full_qkv, preferred_element_type=jnp.float32
    ).astype(jnp.bfloat16)
    key_rows, value_rows = (
        lax.all_gather(projected[1], "ctx", axis=0, tiled=True),
        lax.all_gather(projected[2], "ctx", axis=0, tiled=True),
    )
    key_heads = key_rows.reshape(pack_rows, local_heads, HEAD_DIM)
    value_heads = value_rows.reshape(pack_rows, local_heads, HEAD_DIM)
    query_heads = projected[0].reshape(block_count, block_rows, local_heads, HEAD_DIM)
    context_blocks, log_totals = attend_forward(
        query_heads, seg_mine, key_heads, value_heads, segments
    )
    context = context_blocks.reshape(tok_rows, local_width)
    attn_terms = jnp.dot(context, full_out, preferred_element_type=jnp.float32)
    resid_rows = residual_in + tp_total(attn_terms)
    grad_rows = out_grad.astype(jnp.float32)
    gain_full = full_gains.astype(jnp.float32)
    shift_full = full_shifts.astype(jnp.float32)
    hidden, norm_first = jax.vjp(layer_norm, resid_rows, gain_full[0], shift_full[0])
    hidden_part = hidden.astype(jnp.bfloat16)
    pre_act = jnp.dot(hidden_part, full_up, preferred_element_type=jnp.float32)
    activated, gelu_back = jax.vjp(exact_gelu, pre_act)
    act_low = activated.astype(jnp.bfloat16)
    ffn_terms = jnp.dot(act_low, full_down, preferred_element_type=jnp.float32)
    ffn_rows = tp_total(ffn_terms)
    result, norm_second = jax.vjp(layer_norm, hidden + ffn_rows, gain_full[1], shift_full[1])
    grad_mid, gain_second, shift_second = norm_second(grad_rows)
    mid_part = grad_mid.astype(jnp.bfloat16)
    result_part = result.astype(jnp.bfloat16)
    back_qkv, back_out, back_up, back_down = (
        lax.all_gather(w_qkv, "fsdp", axis=1, tiled=True),
        lax.all_gather(w_out, "fsdp", axis=1, tiled=True),
        lax.all_gather(w_up, "fsdp", axis=0, tiled=True),
        lax.all_gather(w_down, "fsdp", axis=1, tiled=True),
    )
    down_grad = contract_rows(act_low, mid_part)
    act_grad = contract_cols(mid_part, back_down)
    (pre_grad,) = gelu_back(act_grad)
    pre_low = pre_grad.astype(jnp.bfloat16)
    up_grad = contract_rows(hidden_part, pre_low)
    hidden_terms = contract_cols(pre_low, back_up)
    hidden_grad = grad_mid + tp_total(hidden_terms)
    resid_grad, gain_first, shift_first = norm_first(hidden_grad)
    attn_part = resid_grad.astype(jnp.bfloat16)
    out_proj_grad = contract_rows(context, attn_part)
    context_grad = contract_cols(attn_part, back_out).astype(jnp.bfloat16)
    grad_heads = context_grad.reshape(block_count, block_rows, local_heads, HEAD_DIM)
    (key_grad, value_grad), query_grad = attend_backward(
        query_heads, seg_mine, grad_heads, log_totals, key_heads, value_heads, segments
    )
    key_mine, value_mine = (
        lax.psum_scatter(
            key_grad.reshape(pack_rows, local_width), "ctx", scatter_dimension=0, tiled=True
        ),
        lax.psum_scatter(
            value_grad.reshape(pack_rows, local_width), "ctx", scatter_dimension=0, tiled=True
        ),
    )
    proj_grad = jnp.stack(
        [
            query_grad.reshape(tok_rows, local_width).astype(jnp.bfloat16),
            key_mine.astype(jnp.bfloat16),
            value_mine.astype(jnp.bfloat16),
        ]
    )
    qkv_grad = jnp.einsum("td,stc->sdc", tokens, proj_grad, preferred_element_type=jnp.float32)
    input_part = jnp.einsum("stc,sdc->td", proj_grad, back_qkv, preferred_element_type=jnp.float32)
    input_grad = (resid_grad + tp_total(input_part)).astype(jnp.bfloat16)
    gain_grad = jnp.stack([gain_first, gain_second])
    shift_grad = jnp.stack([shift_first, shift_second])
    qkv_grad, out_proj_grad, up_grad, down_grad, gain_grad, shift_grad = (
        lax.psum_scatter(qkv_grad, "fsdp", scatter_dimension=1, tiled=True),
        lax.psum_scatter(out_proj_grad, "fsdp", scatter_dimension=1, tiled=True),
        lax.psum_scatter(up_grad, "fsdp", scatter_dimension=0, tiled=True),
        lax.psum_scatter(down_grad, "fsdp", scatter_dimension=1, tiled=True),
        lax.psum_scatter(gain_grad, "fsdp", scatter_dimension=1, tiled=True),
        lax.psum_scatter(shift_grad, "fsdp", scatter_dimension=1, tiled=True),
    )
    qkv_grad, out_proj_grad, up_grad, down_grad, gain_grad, shift_grad = lax.psum(
        (qkv_grad, out_proj_grad, up_grad, down_grad, gain_grad, shift_grad), "ctx"
    )
    return (
        result_part,
        input_grad,
        qkv_grad,
        out_proj_grad,
        up_grad,
        down_grad,
        gain_grad,
        shift_grad,
    )


def solution(mesh):
    return jax.shard_map(
        body,
        mesh=mesh,
        in_specs=(
            P(("fsdp", "ctx"), None),
            P(None, "fsdp", "tp"),
            P("tp", "fsdp"),
            P("fsdp", "tp"),
            P("tp", "fsdp"),
            P(None, "fsdp"),
            P(None, "fsdp"),
            P("fsdp", None),
            P(("fsdp", "ctx"), None),
        ),
        out_specs=(
            P(("fsdp", "ctx"), None),
            P(("fsdp", "ctx"), None),
            P(None, "fsdp", "tp"),
            P("tp", "fsdp"),
            P("fsdp", "tp"),
            P("tp", "fsdp"),
            P(None, "fsdp"),
            P(None, "fsdp"),
        ),
        check_vma=False,
    )
```

profile of v0, /device:TPU:0, one launch (start us, length us, event | category | flops | bytes accessed | tf_op | source)
XLA Modules:
  0.0 1667.1 jit_solution(5852999273512513464)
XLA Ops:
  9.6 30.5 %all-gather.8.cloned.1.call-done = bf16[3,1024,256]{1,2,0:T(8,128)(2,1)} async-done(((bf16[3,512,256]{1,2,0:T(8,128)(2,1)}), bf16[3,1024,256]{1,2,0:T(8,128)(2,1)}) %all-gather.8.cloned.1.call-update) | async-done | bytes 1572880 | tf_op jit(solution)/shard_map/all_gather | solution.py:111
  55.7 35.5 %all-gather.14.cloned.1.call-done = bf16[1,4096,256]{1,2,0:T(8,128)(2,1)} async-done(((bf16[1,1024,256]{1,2,0:T(8,128)(2,1)}), bf16[1,4096,256]{1,2,0:T(8,128)(2,1)}) %all-gather.14.cloned.1.call-update) | async-done | bytes 2097168 | tf_op jit(solution)/shard_map/all_gather | solution.py:133
  91.2 46.9 %all-gather.16.cloned.1.call-done = bf16[1,4096,256]{1,2,0:T(8,128)(2,1)} async-done(((bf16[1,1024,256]{1,2,0:T(8,128)(2,1)}), bf16[1,4096,256]{1,2,0:T(8,128)(2,1)}) %all-gather.16.cloned.1.call-update) | async-done | bytes 2097168 | tf_op jit(solution)/shard_map/all_gather | solution.py:134
  138.0 99.9 %while.27 = (s32[]{:T(128)}, bf16[2,512,4,64]{1,3,2,0:T(8,128)(2,1)}, f32[2,4,512]{2,1,0:T(4,128)S(1)}, s32[2,512]{1,0:T(2,128)S(1)}, s32[4096]{0:T(1024)S(1)}, ...) while((s32[]{:T(128)}, ...), condition=%wide.region_6.7_spmd, body=%wide.region_2.6_spmd.sunk | while | flops 2271357440 | bytes 113924704 | solution.py:73
  253.3 74.2 %all-reduce.8.cloned.1.call-done = f32[1024,1024]{1,0:T(8,128)} async-done(((f32[1024,1024]{1,0:T(8,128)}), f32[1024,1024]{1,0:T(8,128)}) %all-reduce.8.cloned.1.call-update) | async-done | bytes 4194320 | tf_op jit(solution)/shard_map/psum | solution.py:36
  332.7 29.5 %all-gather.10.cloned.1.call-done = bf16[1024,1024]{1,0:T(8,128)(2,1)} async-done(((bf16[512,1024]{1,0:T(8,128)(2,1)}), bf16[1024,1024]{1,0:T(8,128)(2,1)}) %all-gather.10.cloned.1.call-update) | async-done | bytes 2097168 | tf_op jit(solution)/shard_map/all_gather | solution.py:113
  377.7 19.1 %all-gather.12.cloned.1.call-done = bf16[1024,1024]{1,0:T(8,128)(2,1)} async-done(((bf16[1024,512]{1,0:T(8,128)(2,1)}), bf16[1024,1024]{1,0:T(8,128)(2,1)}) %all-gather.12.cloned.1.call-update) | async-done | bytes 2097168 | tf_op jit(solution)/shard_map/all_gather | solution.py:114
  403.8 85.2 %all-reduce.10.cloned.1.call-done = f32[1024,1024]{1,0:T(8,128)} async-done(((f32[1024,1024]{1,0:T(8,128)}), f32[1024,1024]{1,0:T(8,128)}) %all-reduce.10.cloned.1.call-update) | async-done | bytes 4194320 | tf_op jit(solution)/shard_map/psum | solution.py:36
  513.4 85.7 %all-reduce.12.cloned.1.call-done = f32[1024,1024]{1,0:T(8,128)} async-done(((f32[1024,1024]{1,0:T(8,128)}), f32[1024,1024]{1,0:T(8,128)}) %all-reduce.12.cloned.1.call-update) | async-done | bytes 4194320 | tf_op jit(solution)/shard_map/psum | solution.py:36
  615.2 341.7 %while.28 = (s32[]{:T(128)}, f32[4096,4,64]{0,2,1:T(8,128)}, f32[4096,4,64]{0,2,1:T(8,128)}, bf16[2,512,4,64]{1,3,2,0:T(8,128)(2,1)}, bf16[2,512,4,64]{1,3,2,0:T...) while((s32[]{:T(128)}, f32[4096,4,64]{0,2,1:T(8,128)}, ...), condition=%wide.region_20.21_spmd.clone, body=%wide.region_18.20_spmd.clone.sunk | while | flops 5595217920 | bytes 414817440 | solution.py:104
  644.4 63.5 %fusion.197 = f32[4096,4,64]{0,2,1:T(8,128)} fusion(f32[4,512,4096]{2,1,0:T(8,128)} %fusion.195, f32[4,512,4096]{2,1,0:T(8,128)} %fusion.196, f32[4,512]{1,0:T(4,128)S(1)} %dynamic-slice_bitcast_fusion.2, pred[512,4096]{1,0:T(8,128)(4,1)} %compare_and_fusion.3, f32[4096,4,64]{0,2,1:T(8,128)} %get-tuple-element.498, pred[]{:T(512)S(6)} %compare.3, ...), kind=kOutput, calls=%fused_computation.48.clone.1 | convolution fusion | flops 1168119808 | bytes 147079680 | tf_op jit(solution)/shard_map/while/body/eval_jaxpr/hqk,qhd->khd/dot_general | solution.py:96
  708.0 60.0 %fusion.199 = bf16[2,512,4,64]{1,3,2,0:T(8,128)(2,1)} fusion(bf16[2,512,4,64]{1,3,2,0:T(8,128)(2,1)} %get-tuple-element.500, s32[]{:T(128)} %get-tuple-element.497, bf16[4096,4,64]{0,2,1:T(8,128)(2,1)S(1)} %get-tuple-element.517, f32[4,512,4096]{2,1,0:T(8,128)} %fusion.195, f32[4,512,4096]{2,1,0:T(8,128)} %fusion.196, ...), kind=kOutput, calls=%fused_computation.52.clone.1 | convolution fusion | flops 1166022656 | bytes 141050368 | tf_op jit(solution)/shard_map/while/body/eval_jaxpr/hqk,khd->qhd/dot_general | solution.py:93
  767.9 17.3 %fusion.198 = f32[4096,4,64]{0,2,1:T(8,128)} fusion(f32[4,512,4096]{2,1,0:T(8,128)} %fusion.196, f32[4,512]{1,0:T(4,128)S(1)} %dynamic-slice_bitcast_fusion.2, pred[512,4096]{1,0:T(8,128)(4,1)} %compare_and_fusion.3, f32[4096,4,64]{0,2,1:T(8,128)} %get-tuple-element.499, pred[]{:T(512)S(6)} %compare.3, ...), kind=kOutput, calls=%fused_computation.50.clone.1 | convolution fusion | flops 1109393408 | bytes 44310532 | tf_op jit(solution)/shard_map/while/body/eval_jaxpr/hqk,qhd->khd/dot_general | solution.py:99
  814.3 64.0 %fusion.197 = f32[4096,4,64]{0,2,1:T(8,128)} fusion(f32[4,512,4096]{2,1,0:T(8,128)} %fusion.195, f32[4,512,4096]{2,1,0:T(8,128)} %fusion.196, f32[4,512]{1,0:T(4,128)S(1)} %dynamic-slice_bitcast_fusion.2, pred[512,4096]{1,0:T(8,128)(4,1)} %compare_and_fusion.3, f32[4096,4,64]{0,2,1:T(8,128)} %get-tuple-element.498, pred[]{:T(512)S(6)} %compare.3, ...), kind=kOutput, calls=%fused_computation.48.clone.1 | convolution fusion | flops 1168119808 | bytes 147079680 | tf_op jit(solution)/shard_map/while/body/eval_jaxpr/hqk,qhd->khd/dot_general | solution.py:96
  878.3 60.0 %fusion.199 = bf16[2,512,4,64]{1,3,2,0:T(8,128)(2,1)} fusion(bf16[2,512,4,64]{1,3,2,0:T(8,128)(2,1)} %get-tuple-element.500, s32[]{:T(128)} %get-tuple-element.497, bf16[4096,4,64]{0,2,1:T(8,128)(2,1)S(1)} %get-tuple-element.517, f32[4,512,4096]{2,1,0:T(8,128)} %fusion.195, f32[4,512,4096]{2,1,0:T(8,128)} %fusion.196, ...), kind=kOutput, calls=%fused_computation.52.clone.1 | convolution fusion | flops 1166022656 | bytes 141050368 | tf_op jit(solution)/shard_map/while/body/eval_jaxpr/hqk,khd->qhd/dot_general | solution.py:93
  938.3 18.5 %fusion.198 = f32[4096,4,64]{0,2,1:T(8,128)} fusion(f32[4,512,4096]{2,1,0:T(8,128)} %fusion.196, f32[4,512]{1,0:T(4,128)S(1)} %dynamic-slice_bitcast_fusion.2, pred[512,4096]{1,0:T(8,128)(4,1)} %compare_and_fusion.3, f32[4096,4,64]{0,2,1:T(8,128)} %get-tuple-element.499, pred[]{:T(512)S(6)} %compare.3, ...), kind=kOutput, calls=%fused_computation.50.clone.1 | convolution fusion | flops 1109393408 | bytes 44310532 | tf_op jit(solution)/shard_map/while/body/eval_jaxpr/hqk,qhd->khd/dot_general | solution.py:99
  992.0 47.7 %reduce-scatter.15.cloned.1.call-done = f32[1024,256]{1,0:T(8,128)} async-done(((f32[4096,256]{1,0:T(8,128)}), f32[1024,256]{1,0:T(8,128)}) %reduce-scatter.15.cloned.1.call-update) | async-done | bytes 1048592 | tf_op jit(solution)/shard_map/reduce_scatter | solution.py:184
  1040.9 78.2 %reduce-scatter.13.cloned.1.call-done = f32[1024,256]{1,0:T(8,128)} async-done(((f32[4096,256]{1,0:T(8,128)}), f32[1024,256]{1,0:T(8,128)}) %reduce-scatter.13.cloned.1.call-update) | async-done | bytes 1048592 | tf_op jit(solution)/shard_map/reduce_scatter | solution.py:181
  1142.9 56.5 %reduce-scatter.23.cloned.1.call-done = f32[1024,512]{1,0:T(8,128)} async-done(((f32[1024,1024]{1,0:T(8,128)}), f32[1024,512]{1,0:T(8,128)}) %reduce-scatter.23.cloned.1.call-update) | async-done | bytes 2097168 | tf_op jit(solution)/shard_map/reduce_scatter | solution.py:204
  1199.4 56.7 %reduce-scatter.21.cloned.1.call-done = f32[512,1024]{1,0:T(8,128)} async-done(((f32[1024,1024]{1,0:T(8,128)}), f32[512,1024]{1,0:T(8,128)}) %reduce-scatter.21.cloned.1.call-update) | async-done | bytes 2097168 | tf_op jit(solution)/shard_map/reduce_scatter | solution.py:203
  1256.1 45.5 %reduce-scatter.17.cloned.1.call-done = f32[3,512,256]{1,2,0:T(8,128)} async-done(((f32[3,1024,256]{1,2,0:T(8,128)}), f32[3,512,256]{1,2,0:T(8,128)}) %reduce-scatter.17.cloned.1.call-update) | async-done | bytes 1572880 | tf_op jit(solution)/shard_map/reduce_scatter | solution.py:201
  1301.6 17.3 %reduce-scatter.25.cloned.1.call-done = f32[512,2]{1,0:T(8,128)} async-done(((f32[1024,2]{1,0:T(8,128)}), f32[512,2]{1,0:T(8,128)}) %reduce-scatter.25.cloned.1.call-update) | async-done | bytes 4112
  1349.7 74.4 %all-reduce.14.cloned.1.call-done = f32[1024,1024]{1,0:T(8,128)} async-done(((f32[1024,1024]{1,0:T(8,128)}), f32[1024,1024]{1,0:T(8,128)}) %all-reduce.14.cloned.1.call-update) | async-done | bytes 4194320 | tf_op jit(solution)/shard_map/psum | solution.py:36
  1429.2 221.3 %all-reduce.16.cloned.1.call-done = (f32[3,512,256]{1,2,0:T(8,128)}, f32[256,512]{1,0:T(8,128)}, f32[512,1024]{1,0:T(8,128)}, f32[1024,512]{1,0:T(8,128)}) async-done(((f32[3,512,256]{1,2,0:T(8,128)}, f32[256,512]{1,0:T(8,128)}, f32[512,1024]{1,0:T(8,128)}, f32[1024,512]{1,0:T(8,128)}), (f32[3,512,256]{1,2,0:T(8,128)}, f32[256,512]{1,0:T(8,128)}, f32[512,1024]{1,0:T(8,128)}, ...) | async-done | bytes 6291472 | tf_op jit(solution)/shard_map/psum | solution.py:208
  (226 shorter events, 364.3 us)
Async XLA Ops:
  7.2 32.9 %all-gather.8.cloned.1.call-start = ((), (), s32[]{:S(2)}) async-start(), calls=%async_computation.8 | async-start | bytes 2359296 | tf_op jit(solution)/shard_map/all_gather | solution.py:111
  9.5 81.6 %all-gather.14.cloned.1.call-start = ((), (), s32[]{:S(2)}) async-start(), calls=%async_computation.21 | async-start | bytes 2621440 | tf_op jit(solution)/shard_map/all_gather | solution.py:133
  45.1 92.9 %all-gather.16.cloned.1.call-start = ((), (), s32[]{:S(2)}) async-start(), calls=%async_computation.22 | async-start | bytes 2621440 | tf_op jit(solution)/shard_map/all_gather | solution.py:134
  45.8 281.7 %all-reduce.8.cloned.1.call-start = ((), (), s32[]{:S(2)}) async-start(), calls=%async_computation.9 | async-start | bytes 8388608 | tf_op jit(solution)/shard_map/psum | solution.py:36
  138.0 102.4 %copy-start.11 = (bf16[256,1024]{1,0:T(8,128)(2,1)S(1)}, bf16[256,1024]{1,0:T(8,128)(2,1)}, u32[]{:S(2)}) copy-start(bf16[256,1024]{1,0:T(8,128)(2,1)} %all_gather.31) | copy-start | bytes 1572868
  243.2 119.1 %all-gather.10.cloned.1.call-start = ((), (), s32[]{:S(2)}) async-start(), calls=%async_computation.10 | async-start | bytes 3145728 | tf_op jit(solution)/shard_map/all_gather | solution.py:113
  243.7 153.1 %all-gather.12.cloned.1.call-start = ((), (), s32[]{:S(2)}) async-start(), calls=%async_computation.11 | async-start | bytes 3145728 | tf_op jit(solution)/shard_map/all_gather | solution.py:114
  244.3 244.7 %all-reduce.10.cloned.1.call-start = ((), (), s32[]{:S(2)}) async-start(), calls=%async_computation.12 | async-start | bytes 8388608 | tf_op jit(solution)/shard_map/psum | solution.py:36
  248.7 356.8 %copy-start.21 = (f32[1,1024]{1,0:T(1,128)}, f32[1,1024]{1,0:T(1,128)S(1)}, u32[]{:S(2)}) copy-start(f32[1,1024]{1,0:T(1,128)S(1)} %get-tuple-element.329) | copy-start | bytes 12292
  253.3 235.7 %copy-start.28 = (f32[1,1024]{1,0:T(1,128)}, f32[1,1024]{1,0:T(1,128)S(1)}, u32[]{:S(2)}) copy-start(f32[1,1024]{1,0:T(1,128)S(1)} %get-tuple-element.331) | copy-start | bytes 12292
  330.2 275.3 %copy-start.17 = (f32[1024]{0:T(1024)}, f32[1024]{0:T(1024)S(1)}, u32[]{:S(2)}) copy-start(f32[1024]{0:T(1024)S(1)} %broadcast_multiply_fusion.1) | copy-start | bytes 12292
  332.7 272.8 %copy-start.19 = (f32[1024]{0:T(1024)}, f32[1024]{0:T(1024)S(1)}, u32[]{:S(2)}) copy-start(f32[1024]{0:T(1024)S(1)} %fusion.114) | copy-start | bytes 12292
  403.4 195.7 %all-reduce.12.cloned.1.call-start = ((), (), s32[]{:S(2)}) async-start(), calls=%async_computation.13 | async-start | bytes 8388608 | tf_op jit(solution)/shard_map/psum | solution.py:36
  513.3 526.3 %reduce-scatter.15.cloned.1.call-start = ((), (), s32[]{:S(2)}) async-start(), calls=%async_computation.15 | async-start | bytes 5242880 | tf_op jit(solution)/shard_map/reduce_scatter | solution.py:184
  962.6 156.5 %reduce-scatter.13.cloned.1.call-start = ((), (), s32[]{:S(2)}) async-start(), calls=%async_computation.14 | async-start | bytes 5242880 | tf_op jit(solution)/shard_map/reduce_scatter | solution.py:181
  968.3 174.5 %reduce-scatter.19.cloned.1.call-start = ((), (), s32[]{:S(2)}) async-start(), calls=%async_computation.18 | async-start | bytes 1572864 | tf_op jit(solution)/shard_map/reduce_scatter | solution.py:202
  973.6 225.7 %reduce-scatter.23.cloned.1.call-start = ((), (), s32[]{:S(2)}) async-start(), calls=%async_computation.20 | async-start | bytes 6291456 | tf_op jit(solution)/shard_map/reduce_scatter | solution.py:204
  980.4 275.7 %reduce-scatter.21.cloned.1.call-start = ((), (), s32[]{:S(2)}) async-start(), calls=%async_computation.19 | async-start | bytes 6291456 | tf_op jit(solution)/shard_map/reduce_scatter | solution.py:203
  988.7 132.5 %copy-start.10 = (bf16[1024,1024]{1,0:T(8,128)(2,1)S(1)}, bf16[1024,1024]{1,0:T(8,128)(2,1)}, u32[]{:S(2)}) copy-start(bf16[1024,1024]{1,0:T(8,128)(2,1)} %param.13) | copy-start | bytes 6291460
  988.7 312.8 %reduce-scatter.17.cloned.1.call-start = ((), (), s32[]{:S(2)}) async-start(), calls=%async_computation.17 | async-start | bytes 4718592 | tf_op jit(solution)/shard_map/reduce_scatter | solution.py:201
  1125.8 193.1 %reduce-scatter.25.cloned.1.call-start = ((), (), s32[]{:S(2)}) async-start(), calls=%async_computation.23 | async-start | bytes 786432
  1126.9 209.2 %reduce-scatter.27.cloned.1.call-start = ((), (), s32[]{:S(2)}) async-start(), calls=%async_computation.24 | async-start | bytes 786432
  1128.0 296.0 %all-reduce.14.cloned.1.call-start = ((), (), s32[]{:S(2)}) async-start(), calls=%async_computation.16 | async-start | bytes 8388608 | tf_op jit(solution)/shard_map/psum | solution.py:36
  1133.4 517.1 %all-reduce.16.cloned.1.call-start = ((), (), s32[]{:S(2)}) async-start(), calls=%async_computation.25 | async-start | bytes 12582912 | tf_op jit(solution)/shard_map/psum | solution.py:208
  (38 other events, 316.1 us)
Sparse Core Ops, SparseCore 0:
  10.1 29.8 all-gather.7
  45.2 45.9 all-gather.13
  93.3 44.6 all-gather.15
  243.3 84.1 all-reduce.7
  329.0 33.2 all-gather.9
  363.7 33.1 all-gather.11
  403.5 85.4 all-reduce.9
  513.5 85.6 all-reduce.11
  962.7 76.8 reduce-scatter.14
  1041.8 77.2 reduce-scatter.12
  1122.0 20.8 reduce-scatter.18
  1145.0 54.3 reduce-scatter.22
  1201.8 54.2 reduce-scatter.20
  1258.2 43.3 reduce-scatter.16
  1304.3 14.5 reduce-scatter.24
  1321.6 14.5 reduce-scatter.26
  1338.5 85.4 all-reduce.13
  1426.5 223.9 all-reduce.15
where the time goes:
time: 1670 us
  waiting for transfers between devices  1030 us (62%)
  matrix products  465 us (28%)
  other arithmetic  71.4 us (4%)
  local copies, waits for them, and re-layouts  51.7 us (3%)
  blocking collectives  30.3 us (2%)
    psum x4, waiting for transfers between devices, tp_total(): return lax.psum(terms, 'tp')  319 us
    psum x1, waiting for transfers between devices, body(): lax.psum((qkv_grad, out_proj_grad, up_grad, down_grad, gain_grad, shift_g...  221 us
    dot_general x2, matrix products, one_block(): jnp.einsum('hqk,qhd->khd', grad_scores, query_block, preferred_element_ty...  128 us
    dot_general x2, matrix products, one_block(): jnp.einsum('hqk,khd->qhd', grad_scores, key_heads, preferred_element_type...  120 us
    reduce_scatter x1, waiting for transfers between devices, body(): lax.psum_scatter(key_grad.reshape(pack_rows, local_width), 'ctx', scatter...  78.2 us
    dot_general x4, matrix products, score_block(): jnp.einsum('qhd,khd->hqk', query_block, key_heads, preferred_element_type...  57.8 us
    reduce_scatter x1, waiting for transfers between devices, body(): lax.psum_scatter(up_grad, 'fsdp', scatter_dimension=0, tiled=True)  56.7 us
    reduce_scatter x1, waiting for transfers between devices, body(): lax.psum_scatter(down_grad, 'fsdp', scatter_dimension=1, tiled=True)  56.5 us
  transfers between devices with their start and end apart: 18, of which 18 were waited for; matrix products, arithmetic and copies ran while one was open for 4% of the time, Pallas kernels for 0%

commit v1 on v0

--- a/solution.py
+++ b/solution.py
@@ -33,7 +33,8 @@
 
 
 def tp_total(terms):
-    return lax.psum(terms, "tp")
+    prepare_stops_all = lambda message, axis_key: jnp.sum(lax.all_gather(message, axis_key), 0)
+    return prepare_stops_all(terms, "tp")
 
 
 def segment_of(lengths_row, total):

time: 1670 us -> 1780 us (1.066)
  waiting for transfers between devices: 1030 us -> 1100 us
  other arithmetic: 71.4 us -> 113 us
    all_gather x0 -> x4, waiting for transfers between devices: none -> 410 us  [tp_total(): lax.all_gather(message, axis_key)]
    psum x4 -> x0, waiting for transfers between devices: 319 us -> none  [tp_total(): return lax.psum(terms, 'tp')]
    reduce_sum x0 -> x4, other arithmetic: none -> 41.4 us  [tp_total(): jnp.sum(lax.all_gather(message, axis_key), 0)]
where the time goes in v1:
time: 1780 us; the launch traced here: 1770 us
  waiting for transfers between devices  1100 us (62%)
  matrix products  462 us (26%)
  other arithmetic  113 us (6%)
  local copies, waits for them, and re-layouts  50.6 us (3%)
  blocking collectives  31 us (2%)
    all_gather x4, waiting for transfers between devices, tp_total(): lax.all_gather(message, axis_key)  410 us
    psum x1, waiting for transfers between devices, body(): lax.psum((qkv_grad, out_proj_grad, up_grad, down_grad, gain_grad, shift_g...  213 us
    dot_general x2, matrix products, one_block(): jnp.einsum('hqk,qhd->khd', grad_scores, query_block, preferred_element_ty...  126 us
    dot_general x2, matrix products, one_block(): jnp.einsum('hqk,khd->qhd', grad_scores, key_heads, preferred_element_type...  118 us
    reduce_scatter x1, waiting for transfers between devices, body(): lax.psum_scatter(key_grad.reshape(pack_rows, local_width), 'ctx', scatter...  78.3 us
    dot_general x4, matrix products, score_block(): jnp.einsum('qhd,khd->hqk', query_block, key_heads, preferred_element_type...  57.9 us
    reduce_scatter x1, waiting for transfers between devices, body(): lax.psum_scatter(up_grad, 'fsdp', scatter_dimension=0, tiled=True)  56.6 us
    reduce_scatter x1, waiting for transfers between devices, body(): lax.psum_scatter(down_grad, 'fsdp', scatter_dimension=1, tiled=True)  48.1 us
  transfers between devices with their start and end apart: 18, of which 18 were waited for; matrix products, arithmetic and copies ran while one was open for 4% of the time, Pallas kernels for 0%

profile of v1, /device:TPU:0, one launch (start us, length us, event | category | flops | bytes accessed | tf_op | source)
XLA Modules:
  0.0 1773.4 jit_solution(15968648537390891308)
XLA Ops:
  9.6 30.5 %all-gather.16.cloned.1.call-done = bf16[3,1024,256]{1,2,0:T(8,128)(2,1)} async-done(((bf16[3,512,256]{1,2,0:T(8,128)(2,1)}), bf16[3,1024,256]{1,2,0:T(8,128)(2,1)}) %all-gather.16.cloned.1.call-update) | async-done | bytes 1572880 | tf_op jit(solution)/shard_map/all_gather | solution.py:112
  56.1 35.1 %all-gather.22.cloned.1.call-done = bf16[1,4096,256]{1,2,0:T(8,128)(2,1)} async-done(((bf16[1,1024,256]{1,2,0:T(8,128)(2,1)}), bf16[1,4096,256]{1,2,0:T(8,128)(2,1)}) %all-gather.22.cloned.1.call-update) | async-done | bytes 2097168 | tf_op jit(solution)/shard_map/all_gather | solution.py:134
  91.2 46.9 %all-gather.24.cloned.1.call-done = bf16[1,4096,256]{1,2,0:T(8,128)(2,1)} async-done(((bf16[1,1024,256]{1,2,0:T(8,128)(2,1)}), bf16[1,4096,256]{1,2,0:T(8,128)(2,1)}) %all-gather.24.cloned.1.call-update) | async-done | bytes 2097168 | tf_op jit(solution)/shard_map/all_gather | solution.py:135
  138.0 99.9 %while.27 = (s32[]{:T(128)}, bf16[2,512,4,64]{1,3,2,0:T(8,128)(2,1)}, f32[2,4,512]{2,1,0:T(4,128)S(1)}, s32[2,512]{1,0:T(2,128)S(1)}, s32[4096]{0:T(1024)S(1)}, ...) while((s32[]{:T(128)}, ...), condition=%wide.region_6.7_spmd, body=%wide.region_2.6_spmd.sunk | while | flops 2271357440 | bytes 113924704 | solution.py:74
  253.3 94.7 %all-gather.26.cloned.1.call-done = f32[4096,1024]{1,0:T(8,128)} async-done(((f32[1024,1024]{1,0:T(8,128)}), f32[4096,1024]{1,0:T(8,128)}) %all-gather.26.cloned.1.call-update) | async-done | bytes 16777232 | tf_op jit(solution)/shard_map/all_gather | solution.py:36
  363.8 18.7 %all-gather.18.cloned.1.call-done = bf16[1024,1024]{1,0:T(8,128)(2,1)} async-done(((bf16[512,1024]{1,0:T(8,128)(2,1)}), bf16[1024,1024]{1,0:T(8,128)(2,1)}) %all-gather.18.cloned.1.call-update) | async-done | bytes 2097168 | tf_op jit(solution)/shard_map/all_gather | solution.py:114
  398.0 19.1 %all-gather.20.cloned.1.call-done = bf16[1024,1024]{1,0:T(8,128)(2,1)} async-done(((bf16[1024,512]{1,0:T(8,128)(2,1)}), bf16[1024,1024]{1,0:T(8,128)(2,1)}) %all-gather.20.cloned.1.call-update) | async-done | bytes 2097168 | tf_op jit(solution)/shard_map/all_gather | solution.py:115
  424.1 105.6 %all-gather.28.cloned.1.call-done = f32[4096,1024]{1,0:T(8,128)} async-done(((f32[1024,1024]{1,0:T(8,128)}), f32[4096,1024]{1,0:T(8,128)}) %all-gather.28.cloned.1.call-update) | async-done | bytes 16777232 | tf_op jit(solution)/shard_map/all_gather | solution.py:36
  564.4 106.0 %all-gather.30.cloned.1.call-done = f32[4096,1024]{1,0:T(8,128)} async-done(((f32[1024,1024]{1,0:T(8,128)}), f32[4096,1024]{1,0:T(8,128)}) %all-gather.30.cloned.1.call-update) | async-done | bytes 16777232 | tf_op jit(solution)/shard_map/all_gather | solution.py:36
  696.8 338.4 %while.28 = (s32[]{:T(128)}, f32[4096,4,64]{0,2,1:T(8,128)}, f32[4096,4,64]{0,2,1:T(8,128)}, bf16[2,512,4,64]{1,3,2,0:T(8,128)(2,1)}, bf16[2,512,4,64]{1,3,2,0:T...) while((s32[]{:T(128)}, f32[4096,4,64]{0,2,1:T(8,128)}, ...), condition=%wide.region_20.21_spmd.clone, body=%wide.region_18.20_spmd.clone.sunk | while | flops 5595217920 | bytes 414817440 | solution.py:105
  726.1 62.6 %fusion.197 = f32[4096,4,64]{0,2,1:T(8,128)} fusion(f32[4,512,4096]{2,1,0:T(8,128)} %fusion.195, f32[4,512,4096]{2,1,0:T(8,128)} %fusion.196, f32[4,512]{1,0:T(4,128)S(1)} %dynamic-slice_bitcast_fusion.2, pred[512,4096]{1,0:T(8,128)(4,1)} %compare_and_fusion.3, f32[4096,4,64]{0,2,1:T(8,128)} %get-tuple-element.498, pred[]{:T(512)S(6)} %compare.3, ...), kind=kOutput, calls=%fused_computation.48.clone.1 | convolution fusion | flops 1168119808 | bytes 147079680 | tf_op jit(solution)/shard_map/while/body/eval_jaxpr/hqk,qhd->khd/dot_general | solution.py:97
  788.7 59.2 %fusion.199 = bf16[2,512,4,64]{1,3,2,0:T(8,128)(2,1)} fusion(bf16[2,512,4,64]{1,3,2,0:T(8,128)(2,1)} %get-tuple-element.500, s32[]{:T(128)} %get-tuple-element.497, bf16[4096,4,64]{0,2,1:T(8,128)(2,1)S(1)} %get-tuple-element.517, f32[4,512,4096]{2,1,0:T(8,128)} %fusion.195, f32[4,512,4096]{2,1,0:T(8,128)} %fusion.196, ...), kind=kOutput, calls=%fused_computation.52.clone.1 | convolution fusion | flops 1166022656 | bytes 141050368 | tf_op jit(solution)/shard_map/while/body/eval_jaxpr/hqk,khd->qhd/dot_general | solution.py:94
  848.0 17.3 fusion.198
  894.4 62.9 %fusion.197 = f32[4096,4,64]{0,2,1:T(8,128)} fusion(f32[4,512,4096]{2,1,0:T(8,128)} %fusion.195, f32[4,512,4096]{2,1,0:T(8,128)} %fusion.196, f32[4,512]{1,0:T(4,128)S(1)} %dynamic-slice_bitcast_fusion.2, pred[512,4096]{1,0:T(8,128)(4,1)} %compare_and_fusion.3, f32[4096,4,64]{0,2,1:T(8,128)} %get-tuple-element.498, pred[]{:T(512)S(6)} %compare.3, ...), kind=kOutput, calls=%fused_computation.48.clone.1 | convolution fusion | flops 1168119808 | bytes 147079680 | tf_op jit(solution)/shard_map/while/body/eval_jaxpr/hqk,qhd->khd/dot_general | solution.py:97
  957.3 59.2 %fusion.199 = bf16[2,512,4,64]{1,3,2,0:T(8,128)(2,1)} fusion(bf16[2,512,4,64]{1,3,2,0:T(8,128)(2,1)} %get-tuple-element.500, s32[]{:T(128)} %get-tuple-element.497, bf16[4096,4,64]{0,2,1:T(8,128)(2,1)S(1)} %get-tuple-element.517, f32[4,512,4096]{2,1,0:T(8,128)} %fusion.195, f32[4,512,4096]{2,1,0:T(8,128)} %fusion.196, ...), kind=kOutput, calls=%fused_computation.52.clone.1 | convolution fusion | flops 1166022656 | bytes 141050368 | tf_op jit(solution)/shard_map/while/body/eval_jaxpr/hqk,khd->qhd/dot_general | solution.py:94
  1016.6 18.5 %fusion.198 = f32[4096,4,64]{0,2,1:T(8,128)} fusion(f32[4,512,4096]{2,1,0:T(8,128)} %fusion.196, f32[4,512]{1,0:T(4,128)S(1)} %dynamic-slice_bitcast_fusion.2, pred[512,4096]{1,0:T(8,128)(4,1)} %compare_and_fusion.3, f32[4096,4,64]{0,2,1:T(8,128)} %get-tuple-element.499, pred[]{:T(512)S(6)} %compare.3, ...), kind=kOutput, calls=%fused_computation.50.clone.1 | convolution fusion | flops 1109393408 | bytes 44310532 | tf_op jit(solution)/shard_map/while/body/eval_jaxpr/hqk,qhd->khd/dot_general | solution.py:100
  1072.0 45.9 %reduce-scatter.15.cloned.1.call-done = f32[1024,256]{1,0:T(8,128)} async-done(((f32[4096,256]{1,0:T(8,128)}), f32[1024,256]{1,0:T(8,128)}) %reduce-scatter.15.cloned.1.call-update) | async-done | bytes 1048592 | tf_op jit(solution)/shard_map/reduce_scatter | solution.py:185
  1119.1 78.3 %reduce-scatter.13.cloned.1.call-done = f32[1024,256]{1,0:T(8,128)} async-done(((f32[4096,256]{1,0:T(8,128)}), f32[1024,256]{1,0:T(8,128)}) %reduce-scatter.13.cloned.1.call-update) | async-done | bytes 1048592 | tf_op jit(solution)/shard_map/reduce_scatter | solution.py:182
  1206.5 48.1 %reduce-scatter.23.cloned.1.call-done = f32[1024,512]{1,0:T(8,128)} async-done(((f32[1024,1024]{1,0:T(8,128)}), f32[1024,512]{1,0:T(8,128)}) %reduce-scatter.23.cloned.1.call-update) | async-done | bytes 2097168 | tf_op jit(solution)/shard_map/reduce_scatter | solution.py:205
  1254.5 56.6 %reduce-scatter.21.cloned.1.call-done = f32[512,1024]{1,0:T(8,128)} async-done(((f32[1024,1024]{1,0:T(8,128)}), f32[512,1024]{1,0:T(8,128)}) %reduce-scatter.21.cloned.1.call-update) | async-done | bytes 2097168 | tf_op jit(solution)/shard_map/reduce_scatter | solution.py:204
  1311.1 23.2 %reduce-scatter.19.cloned.1.call-done = f32[256,512]{1,0:T(8,128)} async-done(((f32[256,1024]{1,0:T(8,128)}), f32[256,512]{1,0:T(8,128)}) %reduce-scatter.19.cloned.1.call-update) | async-done | bytes 524304 | tf_op jit(solution)/shard_map/reduce_scatter | solution.py:203
  1334.3 45.6 %reduce-scatter.17.cloned.1.call-done = f32[3,512,256]{1,2,0:T(8,128)} async-done(((f32[3,1024,256]{1,2,0:T(8,128)}), f32[3,512,256]{1,2,0:T(8,128)}) %reduce-scatter.17.cloned.1.call-update) | async-done | bytes 1572880 | tf_op jit(solution)/shard_map/reduce_scatter | solution.py:202
  1428.4 212.6 %all-reduce.4.cloned.1.call-done = (f32[3,512,256]{1,2,0:T(8,128)}, f32[256,512]{1,0:T(8,128)}, f32[512,1024]{1,0:T(8,128)}, f32[1024,512]{1,0:T(8,128)}) async-done(((f32[3,512,256]{1,2,0:T(8,128)}, f32[256,512]{1,0:T(8,128)}, f32[512,1024]{1,0:T(8,128)}, f32[1024,512]{1,0:T(8,128)}), (f32[3,512,256]{1,2,0:T(8,128)}, f32[256,512]{1,0:T(8,128)}, f32[512,1024]{1,0:T(8,128)}, ...) | async-done | bytes 6291472 | tf_op jit(solution)/shard_map/psum | solution.py:209
  1644.0 103.2 %all-gather.32.cloned.1.call-done = f32[4096,1024]{1,0:T(8,128)} async-done(((f32[1024,1024]{1,0:T(8,128)}), f32[4096,1024]{1,0:T(8,128)}) %all-gather.32.cloned.1.call-update) | async-done | bytes 16777232 | tf_op jit(solution)/shard_map/all_gather | solution.py:36
  (234 shorter events, 408.1 us)
Async XLA Ops:
  7.2 32.9 %all-gather.16.cloned.1.call-start = ((), (), s32[]{:S(2)}) async-start(), calls=%async_computation.8 | async-start | bytes 2359296 | tf_op jit(solution)/shard_map/all_gather | solution.py:112
  9.5 81.6 %all-gather.22.cloned.1.call-start = ((), (), s32[]{:S(2)}) async-start(), calls=%async_computation.17 | async-start | bytes 2621440 | tf_op jit(solution)/shard_map/all_gather | solution.py:134
  45.1 92.9 %all-gather.24.cloned.1.call-start = ((), (), s32[]{:S(2)}) async-start(), calls=%async_computation.18 | async-start | bytes 2621440 | tf_op jit(solution)/shard_map/all_gather | solution.py:135
  45.8 302.2 %all-gather.26.cloned.1.call-start = ((), (), s32[]{:S(2)}) async-start(), calls=%async_computation.19 | async-start | bytes 20971520 | tf_op jit(solution)/shard_map/all_gather | solution.py:36
  243.2 139.3 %all-gather.18.cloned.1.call-start = ((), (), s32[]{:S(2)}) async-start(), calls=%async_computation.9 | async-start | bytes 3145728 | tf_op jit(solution)/shard_map/all_gather | solution.py:114
  243.8 173.3 %all-gather.20.cloned.1.call-start = ((), (), s32[]{:S(2)}) async-start(), calls=%async_computation.10 | async-start | bytes 3145728 | tf_op jit(solution)/shard_map/all_gather | solution.py:115
  244.4 285.3 %all-gather.28.cloned.1.call-start = ((), (), s32[]{:S(2)}) async-start(), calls=%async_computation.20 | async-start | bytes 20971520 | tf_op jit(solution)/shard_map/all_gather | solution.py:36
  248.8 438.4 %copy-start.23 = (f32[1,1024]{1,0:T(1,128)}, f32[1,1024]{1,0:T(1,128)S(1)}, u32[]{:S(2)}) copy-start(f32[1,1024]{1,0:T(1,128)S(1)} %get-tuple-element.329) | copy-start | bytes 12292
  253.3 286.7 %copy-start.31 = (f32[1,1024]{1,0:T(1,128)}, f32[1,1024]{1,0:T(1,128)S(1)}, u32[]{:S(2)}) copy-start(f32[1,1024]{1,0:T(1,128)S(1)} %get-tuple-element.331) | copy-start | bytes 12292
  361.2 325.9 %copy-start.19 = (f32[1024]{0:T(1024)}, f32[1024]{0:T(1024)S(1)}, u32[]{:S(2)}) copy-start(f32[1024]{0:T(1024)S(1)} %broadcast_multiply_fusion.1) | copy-start | bytes 12292
  363.8 323.4 %copy-start.21 = (f32[1024]{0:T(1024)}, f32[1024]{0:T(1024)S(1)}, u32[]{:S(2)}) copy-start(f32[1024]{0:T(1024)S(1)} %fusion.114) | copy-start | bytes 12292
  423.6 246.8 %all-gather.30.cloned.1.call-start = ((), (), s32[]{:S(2)}) async-start(), calls=%async_computation.21 | async-start | bytes 20971520 | tf_op jit(solution)/shard_map/all_gather | solution.py:36
  564.3 553.5 %reduce-scatter.15.cloned.1.call-start = ((), (), s32[]{:S(2)}) async-start(), calls=%async_computation.12 | async-start | bytes 5242880 | tf_op jit(solution)/shard_map/reduce_scatter | solution.py:185
  1040.9 156.5 %reduce-scatter.13.cloned.1.call-start = ((), (), s32[]{:S(2)}) async-start(), calls=%async_computation.11 | async-start | bytes 5242880 | tf_op jit(solution)/shard_map/reduce_scatter | solution.py:182
  1046.6 207.9 %reduce-scatter.23.cloned.1.call-start = ((), (), s32[]{:S(2)}) async-start(), calls=%async_computation.16 | async-start | bytes 6291456 | tf_op jit(solution)/shard_map/reduce_scatter | solution.py:205
  1055.4 255.7 %reduce-scatter.21.cloned.1.call-start = ((), (), s32[]{:S(2)}) async-start(), calls=%async_computation.15 | async-start | bytes 6291456 | tf_op jit(solution)/shard_map/reduce_scatter | solution.py:204
  1063.7 270.5 %reduce-scatter.19.cloned.1.call-start = ((), (), s32[]{:S(2)}) async-start(), calls=%async_computation.14 | async-start | bytes 1572864 | tf_op jit(solution)/shard_map/reduce_scatter | solution.py:203
  1068.7 311.1 %reduce-scatter.17.cloned.1.call-start = ((), (), s32[]{:S(2)}) async-start(), calls=%async_computation.13 | async-start | bytes 4718592 | tf_op jit(solution)/shard_map/reduce_scatter | solution.py:202
  1204.1 193.0 %reduce-scatter.25.cloned.1.call-start = ((), (), s32[]{:S(2)}) async-start(), calls=%async_computation.23 | async-start | bytes 786432
  1204.2 175.7 %copy-start.14 = (bf16[1,1024,256]{2,1,0:T(8,128)(2,1)S(1)}, bf16[1,1024,256]{2,1,0:T(8,128)(2,1)}, u32[]{:S(2)}) copy-start(bf16[1,1024,256]{2,1,0:T(8,128)(2,1)} %reshape.362) | copy-start | bytes 1572868
  1204.2 175.7 %copy-start.16 = (bf16[1,1024,256]{2,1,0:T(8,128)(2,1)S(1)}, bf16[1,1024,256]{2,1,0:T(8,128)(2,1)}, u32[]{:S(2)}) copy-start(bf16[1,1024,256]{2,1,0:T(8,128)(2,1)} %copy-done.15) | copy-start | bytes 1572868
  1205.3 209.2 %reduce-scatter.27.cloned.1.call-start = ((), (), s32[]{:S(2)}) async-start(), calls=%async_computation.24 | async-start | bytes 786432
  1206.4 434.5 %all-reduce.4.cloned.1.call-start = ((), (), s32[]{:S(2)}) async-start(), calls=%async_computation.25 | async-start | bytes 12582912 | tf_op jit(solution)/shard_map/psum | solution.py:209
  1379.9 367.3 %all-gather.32.cloned.1.call-start = ((), (), s32[]{:S(2)}) async-start(), calls=%async_computation.22 | async-start | bytes 20971520 | tf_op jit(solution)/shard_map/all_gather | solution.py:36
  (40 other events, 498.5 us)
Sparse Core Ops, SparseCore 0:
  10.1 29.8 all-gather.15
  45.2 45.9 all-gather.21
  93.3 44.6 all-gather.23
  243.3 104.6 all-gather.25
  349.4 33.1 all-gather.17
  383.9 33.1 all-gather.19
  423.7 105.9 all-gather.27
  564.5 105.9 all-gather.29
  1041.1 76.7 reduce-scatter.14
  1120.1 77.2 reduce-scatter.12
  1199.7 54.7 reduce-scatter.22
  1256.8 54.3 reduce-scatter.20
  1313.9 20.3 reduce-scatter.18
  1336.5 43.3 reduce-scatter.16
  1382.5 14.5 reduce-scatter.24
  1399.9 14.5 reduce-scatter.26
  1416.9 223.9 all-reduce.3
  1642.4 104.7 all-gather.31
